TPU v7x, 32 devices: a whole 2x2x4 slice. The times are simulated.
32 devices in a mesh: region: 8 (over y, x, core), member: 4 (over z).
Axes of the slice: x: 2, y: 2, z: 4, core: 2. Of those that a mesh axis runs over, the one named last changes fastest.
Arguments:
- prior_states: float32 [16, 256, 4, 2048], P('region', 'member'), may hold values from -6 to 6
- prior_in_sensor_space: float32 [16, 256, 256], P('region', 'member'), may hold values from -10 to 10
- sensor_readings: float32 [16, 256], replicated, may hold values from -8 to 8
- error_precisions: float32 [16, 256], replicated, may hold values from 0.25 to 4
- live_tallies: int32 [16], replicated, may hold values from 1 to 256
- adjacent_areas: int32 [16, 4], replicated, may hold values from 0 to 15, as said below
- taper_lookup: int32 [16, 5, 256], replicated, may hold values from 0 to 15
- blend_lookup: int32 [16, 4, 5], P('region', 'member'), may hold values from 0 to 15
- taper_factors: float32 [16], replicated, may hold values from 0.05 to 1
Outputs:
- analysis: float32 [16, 256, 4, 2048], P('region', 'member')
Inputs may be any that keep to these rules, and one draw needn't show every extreme that they name: `adjacent_areas`: the 4 neighbours of region r are distinct, differ from r, and each neighbour q satisfies (q // 2 - r // 2) equal to -1, 0 or 1 modulo 16 // 2.
All inputs are finite; a program needn't handle non-finite values.
Results may differ from a plain program's by a relative error of at most 0.0003.
Values sent between devices are 32-bit elements; how exact they have to be, the bound alone decides.
A program may use at most 64 MiB of HBM per device.

v0:
```python
import functools
import jax
import jax.numpy as jnp
from jax import lax
from jax.experimental import pallas as pl
from jax.experimental.pallas import tpu as pltpu
from jax.sharding import PartitionSpec as P

NSIT = 8
LANES = 128
inflation = 1.1
highest = lax.Precision.HIGHEST
MESH = pl.DeviceIdType.MESH


def mm(a, b, dims=(((1,), (0,)), ((), ()))):
    return lax.dot_general(a, b, dims, precision=highest, preferred_element_type=jnp.float32)


def kernel(
    n,
    ring,
    hx_ref,
    read_hbm,
    prec_hbm,
    look_hbm,
    live_hbm,
    adj_hbm,
    blend_hbm,
    taper_hbm,
    x_ref,
    out_ref,
    read_ref,
    prec_ref,
    look_ref,
    live_ref,
    adj_ref,
    blend_ref,
    taper_ref,
    xs,
    ob,
    hxb,
    tb,
    scaled,
    root,
    drive,
    ptt,
    x_send,
    x_recv,
    x_local,
    o_send,
    o_recv,
    o_local,
    h_up,
    h_down,
    h_recv,
    h_local,
    small,
    n_send,
    n_recv,
    t_send,
    t_recv,
):
    me = lax.axis_index("member")
    pos = lax.axis_index("region")
    here = x_ref.shape[0]
    block = x_ref.shape[1]
    cols = x_ref.shape[2]
    members = n * block
    nobs = hx_ref.shape[2]
    blocks = look_ref.shape[0]
    left, right = lax.rem(pos + ring - 1, ring), lax.rem(pos + 1, ring)
    low = me < n // 2

    def partner(i):
        up = n - 1 - i
        return jnp.where(low, jnp.where(up <= me, up - 1, up), jnp.where(i >= me, i + 1, i))

    barrier = pltpu.get_barrier_semaphore()
    for i in range(n - 1):
        pl.semaphore_signal(barrier, inc=1, device_id={"member": partner(i)}, device_id_type=MESH)
    for side in (left, right):
        pl.semaphore_signal(barrier, inc=1, device_id={"region": side}, device_id_type=MESH)
    pl.semaphore_wait(barrier, n + 1)

    def rows(who):
        return pl.ds(pl.multiple_of(who * block, block), block)

    def h_copy(owner, up, own=False):
        kept = hxb.at[pl.ds(here, here), rows(owner)]
        return pltpu.make_async_remote_copy(
            hx_ref if own else kept,
            kept,
            (h_up if up else h_down).at[owner],
            h_recv.at[owner],
            device_id={"member": me + 1 if up else me - 1},
            device_id_type=MESH,
        )

    def h_send(owner, up, act, own=False):
        @pl.when(me < n - 1 if up else me > 0)
        def _():
            getattr(h_copy(owner, up, own), act)()

    def x_copy(r, peer, owner):
        return pltpu.make_async_remote_copy(
            x_ref.at[r, :, :, peer, :],
            xs.at[r, rows(owner)],
            x_send.at[r, peer],
            x_recv.at[r, owner],
            device_id={"member": peer},
            device_id_type=MESH,
        )

    def o_copy(r, peer, owner):
        return pltpu.make_async_remote_copy(
            ob.at[r, rows(peer)],
            out_ref.at[r, :, :, owner, :],
            o_send.at[r, peer],
            o_recv.at[r, owner],
            device_id={"member": peer},
            device_id_type=MESH,
        )

    def beside(buf, send, recv):
        mine = buf.at[pl.ds(here, here)]
        return (
            pltpu.make_async_remote_copy(
                mine,
                buf.at[pl.ds(2 * here, here)],
                send.at[0],
                recv.at[0],
                device_id={"region": left},
                device_id_type=MESH,
            ),
            pltpu.make_async_remote_copy(
                mine,
                buf.at[pl.ds(0, here)],
                send.at[1],
                recv.at[1],
                device_id={"region": right},
                device_id_type=MESH,
            ),
        )

    own_h = pltpu.make_async_copy(hx_ref, hxb.at[pl.ds(here, here), rows(me)], h_local)
    tables = (
        (read_hbm, read_ref),
        (prec_hbm, prec_ref),
        (look_hbm, look_ref),
        (live_hbm, live_ref),
        (adj_hbm, adj_ref),
        (blend_hbm, blend_ref),
        (taper_hbm, taper_ref),
    )
    fetches = [pltpu.make_async_copy(*t, small.at[i]) for i, t in enumerate(tables)]
    own_x = [
        pltpu.make_async_copy(x_ref.at[r, :, :, me, :], xs.at[r, rows(me)], x_local.at[r])
        for r in range(here)
    ]
    h_send(me, True, "start", own=True)
    h_send(me, False, "start", own=True)
    x_copy(0, partner(0), me).start()
    for copy in [own_h] + fetches:
        copy.start()
    for s in range(1, n):
        @pl.when(me - s >= 0)
        def _():
            h_copy(me - s, True).wait_recv()
            h_send(me - s, True, "start")

        @pl.when(me + s < n)
        def _():
            h_copy(me + s, False).wait_recv()
            h_send(me + s, False, "start")

        if s == 1:
            for i in range(1, n - 1):
                x_copy(0, partner(i), me).start()
    for r in range(1, here):
        for i in range(n - 1):
            x_copy(r, partner(i), me).start()
    for copy in own_x:
        copy.start()
    for copy in [own_h] + fetches:
        copy.wait()
    h_pair = beside(hxb, n_send, n_recv)
    for copy in h_pair:
        copy.start()
    for copy in h_pair:
        copy.wait()

    lane = lax.broadcasted_iota(jnp.int32, (1, nobs), 1)
    line = lax.broadcasted_iota(jnp.int32, (members, members), 0)
    cross = lax.broadcasted_iota(jnp.int32, (members, members), 1)
    eye = jnp.where(line == cross, 1.0, 0.0).astype(jnp.float32)
    norms = []

    def area_of(r, b):
        mine = pos * here + r
        return mine if b == 0 else adj_ref[b - 1, mine]

    def slot_of(area):
        slot = lax.rem(area // here - pos + 1 + ring, ring) * here + lax.rem(area, here)
        return jnp.minimum(slot, 3 * here - 1)

    for r in range(here):
        gram = (members - 1) / inflation * eye
        total = jnp.zeros((members, 1), jnp.float32)
        for b in range(blocks):
            area = area_of(r, b)
            looked = look_ref[b, pl.ds(pos * here + r, 1), :]
            taper = jnp.zeros((1, nobs), jnp.float32)
            for level in range(taper_ref.shape[0]):
                taper = jnp.where(looked == level, taper_ref[level], taper)
            live = jnp.where(lane < live_ref[area], prec_ref[pl.ds(area, 1), :], 0.0)
            values = hxb[slot_of(area)]
            mean = jnp.sum(values, axis=0, keepdims=True) * (1.0 / members)
            pert = values - mean
            weighted = pert * (live * taper)
            innovation = read_ref[pl.ds(area, 1), :] - mean
            gram = gram + mm(weighted, pert, (((1,), (1,)), ((), ())))
            total = total + jnp.sum(weighted * innovation, axis=1, keepdims=True)
        norm = jnp.sqrt(
            jnp.sum(jnp.sum(gram * gram, axis=1, keepdims=True), axis=0, keepdims=True)
        )
        norms.append(norm)
        scaled[r] = gram / norm
        root[r] = eye
        drive[r] = jnp.broadcast_to(total, (members, LANES))

    def sweep(step, carry):
        for r in range(here):
            s, t = scaled[r], root[r]
            fix = 1.5 * eye - 0.5 * mm(t, s)
            root[r] = mm(fix, t)
            scaled[r] = mm(s, fix)
        return carry

    lax.fori_loop(0, NSIT, sweep, 0)
    for r in range(here):
        t = root[r]
        shift = mm(t, mm(t, drive[r])) / norms[r]
        factor = jnp.sqrt(jnp.full((1, 1), members - 1.0, jnp.float32)) / jnp.sqrt(norms[r])
        wide = jnp.concatenate([shift] * (members // LANES), axis=1)
        tb[here + r] = factor * t + wide
    t_pair = beside(tb, t_send, t_recv)
    for copy in t_pair:
        copy.start()
    for copy in t_pair:
        copy.wait()
    for r in range(here):
        shares = [taper_ref[blend_ref[r, 0, b]] for b in range(blocks)]
        whole = shares[0]
        for share in shares[1:]:
            whole = whole + share
        mixed = jnp.zeros((members, members), jnp.float32)
        for b in range(blocks):
            mixed = mixed + shares[b] * tb[slot_of(area_of(r, b))]
        ptt[r] = (mixed / jnp.full((1, 1), whole, jnp.float32)).T

    pair = 2
    own_o = []
    for r in range(here):
        own_x[r].wait()
        for i in range(n - 1):
            x_copy(r, me, partner(i)).wait_recv()
        src = xs.at[r].reshape(members * cols, LANES)
        dst = ob.at[r].reshape(members * cols, LANES)

        def update(step, carry, r=r, src=src, dst=dst):
            first = step * pair
            parts = [src[pl.ds(first + c, members, stride=cols), :] for c in range(pair)]
            values = jnp.concatenate(parts, axis=1)
            center = jnp.sum(values, axis=0, keepdims=True) * (1.0 / members)
            new = center + mm(ptt[r], values - center)
            for c in range(pair):
                dst[pl.ds(first + c, members, stride=cols), :] = new[
                    :, c * LANES : (c + 1) * LANES
                ]
            return carry

        lax.fori_loop(0, cols // pair, update, 0)
        for i in range(n - 1):
            o_copy(r, partner(i), me).start()
        mine = pltpu.make_async_copy(ob.at[r, rows(me)], out_ref.at[r, :, :, me, :], o_local.at[r])
        mine.start()
        own_o.append(mine)
    for copy in own_o:
        copy.wait()
    h_send(me, True, "wait_send", own=True)
    h_send(me, False, "wait_send", own=True)
    for s in range(1, n):
        @pl.when(me - s >= 0)
        def _():
            h_send(me - s, True, "wait_send")

        @pl.when(me + s < n)
        def _():
            h_send(me + s, False, "wait_send")

    for r in range(here):
        for i in range(n - 1):
            x_copy(r, partner(i), me).wait_send()
            o_copy(r, partner(i), me).wait_send()
            o_copy(r, me, partner(i)).wait_recv()


def body(
    n,
    ring,
    prior_states,
    prior_in_sensor_space,
    sensor_readings,
    error_precisions,
    live_tallies,
    adjacent_areas,
    taper_lookup,
    blend_lookup,
    taper_factors,
):
    here, block, tiles, points = prior_states.shape
    members = n * block
    nobs = prior_in_sensor_space.shape[2]
    cols = points // LANES
    assert tiles == n and blend_lookup.shape[1] == 1
    x = prior_states.reshape(here, block, tiles, cols, LANES).transpose(0, 1, 3, 2, 4)
    f32 = jnp.float32
    looks, near = taper_lookup.transpose(1, 0, 2), adjacent_areas.T
    dma = pltpu.SemaphoreType.DMA
    out = pl.pallas_call(
        functools.partial(kernel, n, ring),
        out_shape=jax.ShapeDtypeStruct((here, block, cols, n, LANES), f32),
        in_specs=[pl.BlockSpec(memory_space=pltpu.HBM)] * 9,
        out_specs=pl.BlockSpec(memory_space=pl.ANY),
        scratch_shapes=[
            pltpu.VMEM(sensor_readings.shape, f32),
            pltpu.VMEM(error_precisions.shape, f32),
            pltpu.VMEM(looks.shape, jnp.int32),
            pltpu.SMEM(live_tallies.shape, jnp.int32),
            pltpu.SMEM(near.shape, jnp.int32),
            pltpu.SMEM(blend_lookup.shape, jnp.int32),
            pltpu.SMEM(taper_factors.shape, f32),
            pltpu.VMEM((here, members, cols, LANES), f32),
            pltpu.VMEM((here, members, cols, LANES), f32),
            pltpu.VMEM((3 * here, members, nobs), f32),
            pltpu.VMEM((3 * here, members, members), f32),
            pltpu.VMEM((here, members, members), f32),
            pltpu.VMEM((here, members, members), f32),
            pltpu.VMEM((here, members, LANES), f32),
            pltpu.VMEM((here, members, members), f32),
            dma((here, n)),
            dma((here, n)),
            dma((here,)),
            dma((here, n)),
            dma((here, n)),
            dma((here,)),
            dma((n,)),
            dma((n,)),
            dma((n,)),
            dma,
            dma((7,)),
            dma((2,)),
            dma((2,)),
            dma((2,)),
            dma((2,)),
        ],
        compiler_params=pltpu.CompilerParams(
            collective_id=0, has_side_effects=True, vmem_limit_bytes=48 * 1024 * 1024
        ),
        name="letkf",
    )(
        *[
            pltpu.with_memory_space_constraint(a, pltpu.HBM)
            for a in (
                prior_in_sensor_space,
                sensor_readings,
                error_precisions,
                looks,
                live_tallies,
                near,
                blend_lookup,
                taper_factors,
                x,
            )
        ]
    )
    return out.transpose(0, 1, 3, 2, 4).reshape(here, block, tiles, points)


def solution(mesh):
    n, ring = mesh.shape["member"], mesh.shape["region"]
    placed = (
        P("region", "member", None, None),
        P("region", "member", None),
        P(),
        P(),
        P(),
        P(),
        P(),
        P("region", "member", None),
        P(),
    )
    return jax.shard_map(
        functools.partial(body, n, ring),
        mesh=mesh,
        in_specs=placed,
        out_specs=P("region", "member", None, None),
        check_vma=False,
    )
```

profile of v0, /device:TPU:17, one launch (start us, length us, event | category | flops | bytes accessed | tf_op | source)
XLA Modules:
  0.0 190.9 jit_solution(5105757659742415242)
XLA Ops:
  0.0 188.8 %letkf.1 = f32[2,64,16,4,128]{4,3,2,1,0:T(4,128)S(1)} custom-call(f32[2,64,256]{2,1,0:T(8,128)} %hx_ref.1, f32[16,256]{1,0:T(8,128)} %read_hbm.1, f32[16,256]{1,0:T(8,128)} %prec_hbm.1, s32[5,16,256]{2,1,0:T(8,128)} %bitcast.10, s32[16]{0:T(128)} %live_hbm.1, s32[4,16]{1,0:T(4,128)} %bitcast.11, s32[2,1,5]{2,1,0:T(1,128)} %blend_hbm.1, f32[16]{0:T(128)} %taper_hbm.1, ...), custom_call_target="tpu_custom_call" | custom-call | tf_op jit(solution)/shard_map/letkf/pallas_call | solution.py:331
  188.9 2.0 %copy.11 = f32[2,64,4,2048]{3,2,1,0:T(4,128)} copy(f32[2,64,4,2048]{3,2,1,0:T(4,128)S(1)} %bitcast.8) | data formatting | bytes 8388608
where the time goes:
time: 193 us; the launch traced here: 191 us
  Pallas kernels  189 us (98%)
  local copies, waits for them, and re-layouts  2.02 us (1%)
    pallas_call x1, Pallas kernels, body(): pl.pallas_call(functools.partial(kernel, n, ring), out_shape=jax.ShapeDty...  189 us

commit v1 on v0

--- a/solution.py
+++ b/solution.py
@@ -60,6 +60,7 @@
     n_recv,
     t_send,
     t_recv,
+    met,
 ):
     me = lax.axis_index("member")
     pos = lax.axis_index("region")
@@ -70,18 +71,40 @@
     nobs = hx_ref.shape[2]
     blocks = look_ref.shape[0]
     left, right = lax.rem(pos + ring - 1, ring), lax.rem(pos + 1, ring)
-    low = me < n // 2
+    half = n // 2
+    low = me < half
+    inner = jnp.where(low, me + 1, me - 1)
+    outer = jnp.where(low, me - 1, me + 1)
+    middle = (me == half - 1) | (me == half)
+    edge = (me == 0) | (me == n - 1)
 
     def partner(i):
         up = n - 1 - i
         return jnp.where(low, jnp.where(up <= me, up - 1, up), jnp.where(i >= me, i + 1, i))
 
+    def far(i):
+        up = n - 1 - i
+        return jnp.where(low, jnp.where(up < me + 2, up - 2, up), jnp.where(i < me - 1, i, i + 2))
+
+    def tell(sem, **where):
+        pl.semaphore_signal(sem, inc=1, device_id=where, device_id_type=MESH)
+
     barrier = pltpu.get_barrier_semaphore()
-    for i in range(n - 1):
-        pl.semaphore_signal(barrier, inc=1, device_id={"member": partner(i)}, device_id_type=MESH)
-    for side in (left, right):
-        pl.semaphore_signal(barrier, inc=1, device_id={"region": side}, device_id_type=MESH)
-    pl.semaphore_wait(barrier, n + 1)
+
+    @pl.when(middle)
+    def _():
+        tell(barrier, member=inner)
+
+    @pl.when(jnp.logical_not(edge))
+    def _():
+        tell(barrier, member=outer)
+        pl.semaphore_wait(barrier, 1)
+
+    @pl.when(edge)
+    def _():
+        for side in (left, right):
+            tell(barrier, region=side)
+        pl.semaphore_wait(barrier, 3)
 
     def rows(who):
         return pl.ds(pl.multiple_of(who * block, block), block)
@@ -122,26 +145,36 @@
             device_id_type=MESH,
         )
 
-    def beside(buf, send, recv):
-        mine = buf.at[pl.ds(here, here)]
+    def beside(buf, send, recv, part=None, src=None):
+        def at(slot):
+            where = buf.at[pl.ds(slot * here, here)]
+            return where if part is None else where.at[:, rows(part)]
+
+        def sems(ref, side):
+            return ref.at[side] if part is None else ref.at[side, part]
+
+        mine = at(1) if src is None else src
         return (
             pltpu.make_async_remote_copy(
                 mine,
-                buf.at[pl.ds(2 * here, here)],
-                send.at[0],
-                recv.at[0],
+                at(2),
+                sems(send, 0),
+                sems(recv, 0),
                 device_id={"region": left},
                 device_id_type=MESH,
             ),
             pltpu.make_async_remote_copy(
                 mine,
-                buf.at[pl.ds(0, here)],
-                send.at[1],
-                recv.at[1],
+                at(0),
+                sems(send, 1),
+                sems(recv, 1),
                 device_id={"region": right},
                 device_id_type=MESH,
             ),
         )
+
+    def h_beside(owner, src=None):
+        return beside(hxb, n_send, n_recv, owner, src)
 
     own_h = pltpu.make_async_copy(hx_ref, hxb.at[pl.ds(here, here), rows(me)], h_local)
     tables = (
@@ -158,25 +191,90 @@
         pltpu.make_async_copy(x_ref.at[r, :, :, me, :], xs.at[r, rows(me)], x_local.at[r])
         for r in range(here)
     ]
-    h_send(me, True, "start", own=True)
-    h_send(me, False, "start", own=True)
-    x_copy(0, partner(0), me).start()
+    @pl.when(low)
+    def _():
+        h_copy(me, True, True).start()
+
+    @pl.when(jnp.logical_not(low))
+    def _():
+        h_copy(me, False, True).start()
+
+    @pl.when(middle)
+    def _():
+        x_copy(0, inner, me).start()
+
+    @pl.when(jnp.logical_not(edge))
+    def _():
+        pl.semaphore_wait(met.at[0], 1)
+
+    @pl.when(jnp.logical_not(middle))
+    def _():
+        tell(met.at[0], member=inner)
+
+    @pl.when(middle)
+    def _():
+        tell(met.at[1], member=inner)
+
+    pl.semaphore_wait(met.at[1], 1)
+
+    @pl.when(jnp.logical_not(edge))
+    def _():
+        tell(met.at[1], member=outer)
+
+    @pl.when(low & jnp.logical_not(edge))
+    def _():
+        h_copy(me, False, True).start()
+
+    @pl.when(jnp.logical_not(low | edge))
+    def _():
+        h_copy(me, True, True).start()
+
+    @pl.when(jnp.logical_not(middle))
+    def _():
+        x_copy(0, partner(0), me).start()
+
+    @pl.when(edge)
+    def _():
+        tell(met.at[2], region=right)
+        tell(met.at[3], region=left)
+        pl.semaphore_wait(met.at[2], 1)
+        pl.semaphore_wait(met.at[3], 1)
+
+        @pl.when(jnp.logical_not(middle))
+        def _():
+            tell(met.at[4], member=inner)
+
     for copy in [own_h] + fetches:
+        copy.start()
+
+    @pl.when(jnp.logical_not(edge))
+    def _():
+        pl.semaphore_wait(met.at[4], 1)
+
+        @pl.when(jnp.logical_not(middle))
+        def _():
+            tell(met.at[4], member=inner)
+
+    for copy in h_beside(me, hx_ref):
         copy.start()
     for s in range(1, n):
         @pl.when(me - s >= 0)
         def _():
             h_copy(me - s, True).wait_recv()
             h_send(me - s, True, "start")
+            for copy in h_beside(me - s):
+                copy.start()
 
         @pl.when(me + s < n)
         def _():
             h_copy(me + s, False).wait_recv()
             h_send(me + s, False, "start")
+            for copy in h_beside(me + s):
+                copy.start()
 
         if s == 1:
-            for i in range(1, n - 1):
-                x_copy(0, partner(i), me).start()
+            for i in range(n - 2):
+                x_copy(0, jnp.where(middle, far(i), partner(i + 1)), me).start()
     for r in range(1, here):
         for i in range(n - 1):
             x_copy(r, partner(i), me).start()
@@ -184,11 +282,9 @@
         copy.start()
     for copy in [own_h] + fetches:
         copy.wait()
-    h_pair = beside(hxb, n_send, n_recv)
-    for copy in h_pair:
-        copy.start()
-    for copy in h_pair:
-        copy.wait()
+    for owner in range(n):
+        for copy in h_beside(owner):
+            copy.wait()
 
     lane = lax.broadcasted_iota(jnp.int32, (1, nobs), 1)
     line = lax.broadcasted_iota(jnp.int32, (members, members), 0)
@@ -226,18 +322,26 @@
         )
         norms.append(norm)
         scaled[r] = gram / norm
-        root[r] = eye
         drive[r] = jnp.broadcast_to(total, (members, LANES))
+
+    def correction(r):
+        return 1.5 * eye - 0.5 * mm(root[r], scaled[r])
+
+    for r in range(here):
+        fix = 1.5 * eye - 0.5 * scaled[r]
+        root[r] = fix
+        scaled[r] = mm(scaled[r], fix)
 
     def sweep(step, carry):
         for r in range(here):
-            s, t = scaled[r], root[r]
-            fix = 1.5 * eye - 0.5 * mm(t, s)
-            root[r] = mm(fix, t)
-            scaled[r] = mm(s, fix)
+            fix = correction(r)
+            root[r] = mm(fix, root[r])
+            scaled[r] = mm(scaled[r], fix)
         return carry
 
-    lax.fori_loop(0, NSIT, sweep, 0)
+    lax.fori_loop(1, NSIT - 1, sweep, 0)
+    for r in range(here):
+        root[r] = mm(correction(r), root[r])
     for r in range(here):
         t = root[r]
         shift = mm(t, mm(t, drive[r])) / norms[r]
@@ -360,10 +464,11 @@
             dma((n,)),
             dma,
             dma((7,)),
+            dma((2, n)),
+            dma((2, n)),
             dma((2,)),
             dma((2,)),
-            dma((2,)),
-            dma((2,)),
+            pltpu.SemaphoreType.REGULAR((5,)),
         ],
         compiler_params=pltpu.CompilerParams(
             collective_id=0, has_side_effects=True, vmem_limit_bytes=48 * 1024 * 1024

time: 193 us -> 191 us (0.990)
  no operation moved by 1% of the time
where the time goes in v1:
time: 191 us; the launch traced here: 190 us
  Pallas kernels  188 us (98%)
  local copies, waits for them, and re-layouts  2.02 us (1%)
    pallas_call x1, Pallas kernels, body(): pl.pallas_call(functools.partial(kernel, n, ring), out_shape=jax.ShapeDty...  188 us

profile of v1, /device:TPU:17, one launch (start us, length us, event | category | flops | bytes accessed | tf_op | source)
XLA Modules:
  0.0 190.0 jit_solution(7833444893277752025)
XLA Ops:
  0.0 188.0 %letkf.1 = f32[2,64,16,4,128]{4,3,2,1,0:T(4,128)S(1)} custom-call(f32[2,64,256]{2,1,0:T(8,128)} %hx_ref.1, f32[16,256]{1,0:T(8,128)} %read_hbm.1, f32[16,256]{1,0:T(8,128)} %prec_hbm.1, s32[5,16,256]{2,1,0:T(8,128)} %bitcast.10, s32[16]{0:T(128)} %live_hbm.1, s32[4,16]{1,0:T(4,128)} %bitcast.11, s32[2,1,5]{2,1,0:T(1,128)} %blend_hbm.1, f32[16]{0:T(128)} %taper_hbm.1, ...), custom_call_target="tpu_custom_call" | custom-call | tf_op jit(solution)/shard_map/letkf/pallas_call | solution.py:435
  188.0 2.0 %copy.11 = f32[2,64,4,2048]{3,2,1,0:T(4,128)} copy(f32[2,64,4,2048]{3,2,1,0:T(4,128)S(1)} %bitcast.8) | data formatting | bytes 8388608

commit v2 on v1

--- a/solution.py
+++ b/solution.py
@@ -11,6 +11,21 @@
 inflation = 1.1
 highest = lax.Precision.HIGHEST
 MESH = pl.DeviceIdType.MESH
+
+
+def late_cols(cols):
+    return 0, max(3 * cols // 8, 1)
+
+
+def partner_of(me, n, i):
+    up = n - 1 - i
+    low = jnp.where(up <= me, up - 1, up)
+    return jnp.where(me < n // 2, low, jnp.where(i >= me, i + 1, i))
+
+
+def by_core(act):
+    for core in range(2):
+        pl.when(lax.rem(lax.axis_index("region"), 2) == core)(functools.partial(act, core))
 
 
 def mm(a, b, dims=(((1,), (0,)), ((), ()))):
@@ -30,6 +45,7 @@
     taper_hbm,
     x_ref,
     out_ref,
+    late_ref,
     read_ref,
     prec_ref,
     look_ref,
@@ -51,6 +67,7 @@
     o_send,
     o_recv,
     o_local,
+    late_sem,
     h_up,
     h_down,
     h_recv,
@@ -79,8 +96,7 @@
     edge = (me == 0) | (me == n - 1)
 
     def partner(i):
-        up = n - 1 - i
-        return jnp.where(low, jnp.where(up <= me, up - 1, up), jnp.where(i >= me, i + 1, i))
+        return partner_of(me, n, i)
 
     def far(i):
         up = n - 1 - i
@@ -135,15 +151,22 @@
             device_id_type=MESH,
         )
 
-    def o_copy(r, peer, owner):
+    def o_copy(r, peer, owner, upto):
+        part = pl.ds(0, upto)
         return pltpu.make_async_remote_copy(
-            ob.at[r, rows(peer)],
-            out_ref.at[r, :, :, owner, :],
+            ob.at[r, rows(peer), part],
+            out_ref.at[r, :, part, owner, :],
             o_send.at[r, peer],
             o_recv.at[r, owner],
             device_id={"member": peer},
             device_id_type=MESH,
         )
+
+    def o_each(r, act):
+        if r < here - 1:
+            act(cols)
+        else:
+            by_core(lambda core: act(cols - late_cols(cols)[core]))
 
     def beside(buf, send, recv, part=None, src=None):
         def at(slot):
@@ -385,12 +408,21 @@
             return carry
 
         lax.fori_loop(0, cols // pair, update, 0)
-        for i in range(n - 1):
-            o_copy(r, partner(i), me).start()
+
+        def o_start(upto, r=r):
+            for i in range(n - 1):
+                o_copy(r, partner(i), me, upto).start()
+
+        o_each(r, o_start)
         mine = pltpu.make_async_copy(ob.at[r, rows(me)], out_ref.at[r, :, :, me, :], o_local.at[r])
         mine.start()
         own_o.append(mine)
-    for copy in own_o:
+    wide = late_ref.shape[1]
+    late = pltpu.make_async_copy(
+        ob.at[here - 1, :, pl.ds(cols - wide, wide)], late_ref, late_sem
+    )
+    late.start()
+    for copy in own_o + [late]:
         copy.wait()
     h_send(me, True, "wait_send", own=True)
     h_send(me, False, "wait_send", own=True)
@@ -406,8 +438,93 @@
     for r in range(here):
         for i in range(n - 1):
             x_copy(r, partner(i), me).wait_send()
-            o_copy(r, partner(i), me).wait_send()
-            o_copy(r, me, partner(i)).wait_recv()
+
+        def o_wait(upto, r=r):
+            for i in range(n - 1):
+                o_copy(r, partner(i), me, upto).wait_send()
+                o_copy(r, me, partner(i), upto).wait_recv()
+
+        o_each(r, o_wait)
+
+
+def keep(land_ref, out_ref, sems):
+    here, cols = land_ref.shape[0], land_ref.shape[2]
+
+    def move(core):
+        copies = []
+        for r in range(here):
+            upto = cols if r < here - 1 else cols - late_cols(cols)[core]
+            part = pl.ds(0, upto)
+            copies.append(
+                pltpu.make_async_copy(
+                    land_ref.at[r, :, part], out_ref.at[r, :, part], sems.at[r]
+                )
+            )
+        for copy in copies:
+            copy.start()
+        for copy in copies:
+            copy.wait()
+
+    by_core(move)
+
+
+def rest(n, cols, late_ref, kept_ref, out_ref, send, recv, local):
+    me = lax.axis_index("member")
+    block, wide = out_ref.shape[0], out_ref.shape[1]
+
+    def rows(who):
+        return pl.ds(pl.multiple_of(who * block, block), block)
+
+    def move(core):
+        some = late_cols(cols)[core]
+        if some == 0:
+            return
+        barrier = pltpu.get_barrier_semaphore()
+        for i in range(n - 1):
+            pl.semaphore_signal(
+                barrier, inc=1, device_id={"member": partner_of(me, n, i)}, device_id_type=MESH
+            )
+        pl.semaphore_wait(barrier, n - 1)
+        part = pl.ds(wide - some, some)
+
+        def copy(peer, owner):
+            return pltpu.make_async_remote_copy(
+                late_ref.at[rows(peer), part],
+                out_ref.at[:, part, owner, :],
+                send.at[peer],
+                recv.at[owner],
+                device_id={"member": peer},
+                device_id_type=MESH,
+            )
+
+        mine = pltpu.make_async_copy(late_ref.at[rows(me), part], out_ref.at[:, part, me, :], local)
+        for i in range(n - 1):
+            copy(partner_of(me, n, i), me).start()
+        mine.start()
+        mine.wait()
+        for i in range(n - 1):
+            copy(partner_of(me, n, i), me).wait_send()
+            copy(me, partner_of(me, n, i)).wait_recv()
+
+    by_core(move)
+
+
+def join(land_ref, kept_ref, out_ref, sem):
+    here, cols, wide = out_ref.shape[0], out_ref.shape[2], land_ref.shape[1]
+
+    def move(core):
+        some = late_cols(cols)[core]
+        if some == 0:
+            return
+        copy = pltpu.make_async_copy(
+            land_ref.at[:, pl.ds(wide - some, some)],
+            out_ref.at[here - 1, :, pl.ds(cols - some, some)],
+            sem,
+        )
+        copy.start()
+        copy.wait()
+
+    by_core(move)
 
 
 def body(
@@ -432,11 +549,16 @@
     f32 = jnp.float32
     looks, near = taper_lookup.transpose(1, 0, 2), adjacent_areas.T
     dma = pltpu.SemaphoreType.DMA
-    out = pl.pallas_call(
+    whole = jax.ShapeDtypeStruct((here, block, cols, n, LANES), f32)
+    wide = max(late_cols(cols))
+    hbm = functools.partial(pltpu.with_memory_space_constraint, memory_space=pltpu.HBM)
+    in_hbm, anywhere = pl.BlockSpec(memory_space=pltpu.HBM), pl.BlockSpec(memory_space=pl.ANY)
+    few = 4 * 1024 * 1024
+    land, late = pl.pallas_call(
         functools.partial(kernel, n, ring),
-        out_shape=jax.ShapeDtypeStruct((here, block, cols, n, LANES), f32),
+        out_shape=(whole, jax.ShapeDtypeStruct((members, wide, LANES), f32)),
         in_specs=[pl.BlockSpec(memory_space=pltpu.HBM)] * 9,
-        out_specs=pl.BlockSpec(memory_space=pl.ANY),
+        out_specs=(anywhere, anywhere),
         scratch_shapes=[
             pltpu.VMEM(sensor_readings.shape, f32),
             pltpu.VMEM(error_precisions.shape, f32),
@@ -459,6 +581,7 @@
             dma((here, n)),
             dma((here, n)),
             dma((here,)),
+            dma,
             dma((n,)),
             dma((n,)),
             dma((n,)),
@@ -471,7 +594,7 @@
             pltpu.SemaphoreType.REGULAR((5,)),
         ],
         compiler_params=pltpu.CompilerParams(
-            collective_id=0, has_side_effects=True, vmem_limit_bytes=48 * 1024 * 1024
+            collective_id=0, has_side_effects=True, vmem_limit_bytes=40 * 1024 * 1024
         ),
         name="letkf",
     )(
@@ -490,6 +613,37 @@
             )
         ]
     )
+    kept = pl.pallas_call(
+        keep,
+        out_shape=whole,
+        in_specs=[anywhere],
+        out_specs=in_hbm,
+        scratch_shapes=[dma((here,))],
+        compiler_params=pltpu.CompilerParams(vmem_limit_bytes=few),
+        name="keep",
+    )(land)
+    kept = hbm(kept)
+    last = pl.pallas_call(
+        functools.partial(rest, n, cols),
+        out_shape=jax.ShapeDtypeStruct((block, wide, n, LANES), f32),
+        in_specs=[anywhere, in_hbm],
+        out_specs=anywhere,
+        scratch_shapes=[dma((n,)), dma((n,)), dma],
+        compiler_params=pltpu.CompilerParams(
+            collective_id=1, has_side_effects=True, vmem_limit_bytes=few
+        ),
+        name="rest",
+    )(late, kept)
+    out = pl.pallas_call(
+        join,
+        out_shape=whole,
+        in_specs=[anywhere, in_hbm],
+        out_specs=in_hbm,
+        input_output_aliases={1: 0},
+        scratch_shapes=[dma],
+        compiler_params=pltpu.CompilerParams(vmem_limit_bytes=few),
+        name="join",
+    )(last, kept)
     return out.transpose(0, 1, 3, 2, 4).reshape(here, block, tiles, points)
 
 

time: 191 us -> 189 us (0.990)
  local copies, waits for them, and re-layouts: 2.02 us -> 0 us
    unnamed x1 -> x0, local copies, waits for them, and re-layouts: 2.02 us -> none
    pallas_call x1 -> x4, Pallas kernels: 188 us -> 189 us  [the longest x1 175 us: body(): pl.pallas_call(functools.partial(kernel, n, ring), out_shape=(whole, jax....]
where the time goes in v2:
time: 189 us
  Pallas kernels  189 us (100%)
    pallas_call x1, Pallas kernels, body(): pl.pallas_call(functools.partial(kernel, n, ring), out_shape=(whole, jax....  175 us
    pallas_call x1, Pallas kernels, body(): pl.pallas_call(functools.partial(rest, n, cols), out_shape=jax.ShapeDtype...  11.1 us

profile of v2, /device:TPU:17, one launch (start us, length us, event | category | flops | bytes accessed | tf_op | source)
XLA Modules:
  0.0 189.1 jit_solution(6101331638344589956)
XLA Ops:
  0.0 175.3 %letkf.1 = (f32[2,64,16,4,128]{4,3,2,1,0:T(4,128)S(1)}, f32[256,6,128]{2,1,0:T(8,128)S(1)}) custom-call(f32[2,64,256]{2,1,0:T(8,128)} %hx_ref.1, f32[16,256]{1,0:T(8,128)} %read_hbm.1, f32[16,256]{1,0:T(8,128)} %prec_hbm.1, s32[5,16,256]{2,1,0:T(8,128)} %bitcast.9, s32[16]{0:T(128)} %live_hbm.1, s32[4,16]{1,0:T(4,128)} %bitcast.10, s32[2,1,5]{2,1,0:T(1,128)} %blend_hbm.1, ...), custom_call_target="tpu_custom_call" | custom-call | tf_op jit(solution)/shard_map/letkf/pallas_call | solution.py:557
  175.4 1.8 keep.1.kept_ref
  177.1 11.1 %rest.1.land_ref = f32[64,6,4,128]{3,2,1,0:T(4,128)S(1)} custom-call(f32[256,6,128]{2,1,0:T(8,128)S(1)} %get-tuple-element.7.late_ref, f32[2,64,16,4,128]{4,3,2,1,0:T(4,128)} %keep.1.kept_ref), custom_call_target="tpu_custom_call" | custom-call | tf_op jit(solution)/shard_map/rest/pallas_call | solution.py:626
  188.2 0.9 join.1
